TPU v7x, 32 devices: a whole 2x2x4 slice. The times are simulated.
32 devices in a mesh: dp: 8 (over z, x), seq: 4 (over y, core).
Axes of the slice: x: 2, y: 2, z: 4, core: 2. Of those that a mesh axis runs over, the one named last changes fastest.
Arguments:
- captions: bfloat16 [96, 128, 768], P(('dp', 'seq')), may hold values from -6 to 6
- images: bfloat16 [96, 196, 768], P('dp'), may hold values from -6 to 6
- tissue_mask: int32 [96, 196], P('dp'), may hold values from 0 to 1, as said below
- gain_self: bfloat16 [768], P(('dp', 'seq')), may hold values from 0.5 to 1.5
- gain_cross: bfloat16 [768], P(('dp', 'seq')), may hold values from 0.5 to 1.5
- gain_mlp: bfloat16 [768], P(('dp', 'seq')), may hold values from 0.5 to 1.5
- w_qkv: bfloat16 [768, 2304], P(('dp', 'seq')), may hold values from -0.21875 to 0.21875
- w_self_out: bfloat16 [768, 768], P(('dp', 'seq')), may hold values from -0.625 to 0.625
- w_cross_q: bfloat16 [768, 768], P(('dp', 'seq')), may hold values from -0.21875 to 0.21875
- w_cross_kv: bfloat16 [768, 1536], P(('dp', 'seq')), may hold values from -0.21875 to 0.21875
- w_cross_out: bfloat16 [768, 768], P(('dp', 'seq')), may hold values from -0.625 to 0.625
- w_up: bfloat16 [768, 3072], P(('dp', 'seq')), may hold values from -0.21875 to 0.21875
- w_down: bfloat16 [3072, 768], P(('dp', 'seq')), may hold values from -0.109375 to 0.109375
- cotangent: bfloat16 [96, 128, 768], P(('dp', 'seq')), may hold values from -6 to 6
Outputs:
- block_out: bfloat16 [96, 128, 768], P(('dp', 'seq'))
- grad_captions: float32 [96, 128, 768], P(('dp', 'seq'))
- grad_images: float32 [96, 196, 768], P('dp', None, 'seq')
- grad_gain_self: float32 [768], P(('dp', 'seq'))
- grad_gain_cross: float32 [768], P(('dp', 'seq'))
- grad_gain_mlp: float32 [768], P(('dp', 'seq'))
- grad_w_qkv: float32 [768, 2304], P(('dp', 'seq'))
- grad_w_self_out: float32 [768, 768], P(('dp', 'seq'))
- grad_w_cross_q: float32 [768, 768], P(('dp', 'seq'))
- grad_w_cross_kv: float32 [768, 1536], P(('dp', 'seq'))
- grad_w_cross_out: float32 [768, 768], P(('dp', 'seq'))
- grad_w_up: float32 [768, 3072], P(('dp', 'seq'))
- grad_w_down: float32 [3072, 768], P(('dp', 'seq'))
Inputs may be any that keep to these rules, and one draw needn't show every extreme that they name: `tissue_mask`: at least 65 of every image's patches are valid; the valid ones lie anywhere among its 196 slots and their number differs from image to image.
All inputs are finite; a program needn't handle non-finite values.
Results may differ from a plain program's by a relative error of at most 0.019.
Values may be sent and summed in bfloat16 or wider, within the bound.
A program may use at most 192 MiB of HBM per device.

v0:
```python
import jax
import jax.numpy as jnp
from jax import lax
from jax.sharding import PartitionSpec as P

HEADS = 12
HEAD = 64
epsilon = 1e-05


def layer_norm(inputs, gain_vector):
    centered = inputs - jnp.mean(inputs, axis=-1, keepdims=True)
    spread = jnp.mean(centered * centered, axis=-1, keepdims=True)
    return centered * lax.rsqrt(spread + epsilon) * gain_vector


def norm_back(inputs, gain_vector, upstream):
    unused, pullback = jax.vjp(layer_norm, inputs, gain_vector)
    return pullback(upstream)


def exact_gelu(inputs):
    return jax.nn.gelu(inputs, approximate=False)


def linear(inputs, matrix):
    return jnp.einsum("btd,de->bte", inputs, matrix, preferred_element_type=jnp.float32)


def linear_back(upstream, matrix):
    return jnp.einsum("bte,de->btd", upstream, matrix, preferred_element_type=jnp.float32)


def weight_grad(inputs, upstream):
    return jnp.einsum("btd,bte->de", inputs, upstream, preferred_element_type=jnp.float32)


def masked_scores(query_heads, key_heads, allowed, factor):
    raw_scores = (
        jnp.einsum("bqhe,bkhe->bhqk", query_heads, key_heads, preferred_element_type=jnp.float32)
        * factor
    )
    return jnp.where(allowed, raw_scores, -1e30)


def attend_forward(query_heads, key_heads, value_heads, allowed, factor):
    scores = masked_scores(query_heads, key_heads, allowed, factor)
    top_score = jnp.max(scores, axis=-1, keepdims=True)
    exponent = jnp.exp(scores - top_score)
    totals = jnp.sum(exponent, axis=-1, keepdims=True)
    probabilities = (exponent / totals).astype(jnp.bfloat16)
    attended = jnp.einsum(
        "bhqk,bkhe->bqhe", probabilities, value_heads, preferred_element_type=jnp.float32
    )
    return (attended.astype(jnp.bfloat16), top_score + jnp.log(totals))


def attend_back(query_heads, key_heads, value_heads, allowed, factor, log_totals, upstream):
    probabilities = jnp.exp(masked_scores(query_heads, key_heads, allowed, factor) - log_totals)
    grad_probs = jnp.einsum(
        "bqhe,bkhe->bhqk", upstream, value_heads, preferred_element_type=jnp.float32
    )
    centered = grad_probs - jnp.sum(grad_probs * probabilities, axis=-1, keepdims=True)
    grad_scores = (probabilities * centered * factor).astype(jnp.bfloat16)
    grad_queries = jnp.einsum(
        "bhqk,bkhe->bqhe", grad_scores, key_heads, preferred_element_type=jnp.float32
    )
    grad_keys = jnp.einsum(
        "bhqk,bqhe->bkhe", grad_scores, query_heads, preferred_element_type=jnp.float32
    )
    grad_values = jnp.einsum(
        "bhqk,bqhe->bkhe",
        probabilities.astype(jnp.bfloat16),
        upstream,
        preferred_element_type=jnp.float32,
    )
    return (
        grad_queries.astype(jnp.bfloat16),
        grad_keys.astype(jnp.bfloat16),
        grad_values.astype(jnp.bfloat16),
    )


def pair_columns(full_cross_kv, seq_index, head_span, model_width):
    key_cols = lax.dynamic_slice_in_dim(full_cross_kv, seq_index * head_span, head_span, 1)
    value_cols = lax.dynamic_slice_in_dim(
        full_cross_kv, model_width + seq_index * head_span, head_span, 1
    )
    return jnp.concatenate([key_cols, value_cols], axis=1)


def on_device(
    captions,
    images,
    tissue_mask,
    gain_self,
    gain_cross,
    gain_mlp,
    w_qkv,
    w_self_out,
    w_cross_q,
    w_cross_kv,
    w_cross_out,
    w_up,
    w_down,
    cotangent,
):
    groups = lax.axis_size("seq")
    seq_index = lax.axis_index("seq")
    count_local, full_len, model_width = captions.shape
    count_caps = count_local * groups
    patch_count = images.shape[1]
    local_heads = HEADS // groups
    head_span = local_heads * HEAD
    factor = HEAD ** (-0.5)
    gathered = (
        lax.all_gather(gain_self, ("dp", "seq"), axis=0, tiled=True),
        lax.all_gather(gain_cross, ("dp", "seq"), axis=0, tiled=True),
        lax.all_gather(gain_mlp, ("dp", "seq"), axis=0, tiled=True),
        lax.all_gather(w_qkv, ("dp", "seq"), axis=0, tiled=True),
        lax.all_gather(w_self_out, ("dp", "seq"), axis=0, tiled=True),
        lax.all_gather(w_cross_q, ("dp", "seq"), axis=0, tiled=True),
        lax.all_gather(w_cross_kv, ("dp", "seq"), axis=0, tiled=True),
        lax.all_gather(w_cross_out, ("dp", "seq"), axis=0, tiled=True),
        lax.all_gather(w_up, ("dp", "seq"), axis=0, tiled=True),
        lax.all_gather(w_down, ("dp", "seq"), axis=0, tiled=True),
    )
    (
        gain_one,
        gain_two,
        gain_three,
        full_qkv,
        full_self_out,
        full_cross_q,
        full_cross_kv,
        full_cross_out,
        full_up,
        full_down,
    ) = gathered
    position = jnp.arange(full_len)
    causal = (position[:, None] >= position[None, :])[None, None]
    split_shape = (count_local, full_len, groups, head_span)
    head_shape = (count_caps, full_len, local_heads, HEAD)
    back_shape = (count_caps, full_len, 1, head_span)
    token_shape = (count_local, full_len, model_width)
    tokens = captions.astype(jnp.float32)
    normed_one = layer_norm(tokens, gain_one.astype(jnp.float32)).astype(jnp.bfloat16)
    packed = linear(normed_one, full_qkv).astype(jnp.bfloat16)
    query_part = packed[..., :model_width].reshape(split_shape)
    key_part = packed[..., model_width : 2 * model_width].reshape(split_shape)
    value_part = packed[..., 2 * model_width :].reshape(split_shape)
    query_recv, key_recv, value_recv = (
        lax.all_to_all(query_part, "seq", split_axis=2, concat_axis=0, tiled=True),
        lax.all_to_all(key_part, "seq", split_axis=2, concat_axis=0, tiled=True),
        lax.all_to_all(value_part, "seq", split_axis=2, concat_axis=0, tiled=True),
    )
    query_heads = query_recv.reshape(head_shape)
    key_heads = key_recv.reshape(head_shape)
    value_heads = value_recv.reshape(head_shape)
    self_result, self_totals = attend_forward(query_heads, key_heads, value_heads, causal, factor)
    self_back = lax.all_to_all(
        self_result.reshape(back_shape), "seq", split_axis=0, concat_axis=2, tiled=True
    )
    self_tokens = self_back.reshape(token_shape)
    after_self = tokens + linear(self_tokens, full_self_out)
    normed_two = layer_norm(after_self, gain_two.astype(jnp.float32)).astype(jnp.bfloat16)
    cross_full = linear(normed_two, full_cross_q).astype(jnp.bfloat16)
    cross_queries = lax.all_to_all(
        cross_full.reshape(split_shape), "seq", split_axis=2, concat_axis=0, tiled=True
    ).reshape(head_shape)
    image_allowed = (tissue_mask > 0)[:, None, None, :]
    local_pairs = pair_columns(full_cross_kv, seq_index, head_span, model_width)
    image_pairs = linear(images, local_pairs).astype(jnp.bfloat16)
    image_shape = (count_caps, patch_count, local_heads, HEAD)
    cross_keys = image_pairs[..., :head_span].reshape(image_shape)
    cross_values = image_pairs[..., head_span:].reshape(image_shape)
    cross_result, cross_totals = attend_forward(
        cross_queries, cross_keys, cross_values, image_allowed, factor
    )
    cross_back = lax.all_to_all(
        cross_result.reshape(back_shape), "seq", split_axis=0, concat_axis=2, tiled=True
    )
    cross_tokens = cross_back.reshape(token_shape)
    after_cross = after_self + linear(cross_tokens, full_cross_out)
    normed_three = layer_norm(after_cross, gain_three.astype(jnp.float32)).astype(jnp.bfloat16)
    hidden = linear(normed_three, full_up)
    active = exact_gelu(hidden).astype(jnp.bfloat16)
    block_out = (after_cross + linear(active, full_down)).astype(jnp.bfloat16)
    backward_set = (
        lax.all_gather(gain_self, ("dp", "seq"), axis=0, tiled=True),
        lax.all_gather(gain_cross, ("dp", "seq"), axis=0, tiled=True),
        lax.all_gather(gain_mlp, ("dp", "seq"), axis=0, tiled=True),
        lax.all_gather(w_qkv, ("dp", "seq"), axis=0, tiled=True),
        lax.all_gather(w_self_out, ("dp", "seq"), axis=0, tiled=True),
        lax.all_gather(w_cross_q, ("dp", "seq"), axis=0, tiled=True),
        lax.all_gather(w_cross_kv, ("dp", "seq"), axis=0, tiled=True),
        lax.all_gather(w_cross_out, ("dp", "seq"), axis=0, tiled=True),
        lax.all_gather(w_up, ("dp", "seq"), axis=0, tiled=True),
        lax.all_gather(w_down, ("dp", "seq"), axis=0, tiled=True),
    )
    (
        gain_one,
        gain_two,
        gain_three,
        full_qkv,
        full_self_out,
        full_cross_q,
        full_cross_kv,
        full_cross_out,
        full_up,
        full_down,
    ) = backward_set
    grad_down = weight_grad(active, cotangent)
    grad_active = linear_back(cotangent, full_down)
    unused, gelu_pull = jax.vjp(exact_gelu, hidden)
    grad_hidden = gelu_pull(grad_active)[0].astype(jnp.bfloat16)
    grad_up = weight_grad(normed_three, grad_hidden)
    grad_normed_three = linear_back(grad_hidden, full_up)
    norm_grad_three, grad_gain_three = norm_back(
        after_cross, gain_three.astype(jnp.float32), grad_normed_three
    )
    grad_after_cross = cotangent.astype(jnp.float32) + norm_grad_three
    cross_branch = grad_after_cross.astype(jnp.bfloat16)
    grad_cross_out = weight_grad(cross_tokens, cross_branch)
    cross_full_grad = linear_back(cross_branch, full_cross_out).astype(jnp.bfloat16)
    cross_upstream = lax.all_to_all(
        cross_full_grad.reshape(split_shape), "seq", split_axis=2, concat_axis=0, tiled=True
    ).reshape(head_shape)
    grad_cross_queries, grad_cross_keys, grad_cross_values = attend_back(
        cross_queries, cross_keys, cross_values, image_allowed, factor, cross_totals, cross_upstream
    )
    pair_grads = jnp.concatenate(
        [
            grad_cross_keys.reshape(count_caps, patch_count, head_span),
            grad_cross_values.reshape(count_caps, patch_count, head_span),
        ],
        axis=-1,
    )
    local_pairs = pair_columns(full_cross_kv, seq_index, head_span, model_width)
    grad_local_pairs = weight_grad(images, pair_grads)
    image_terms = linear_back(pair_grads, local_pairs)
    grad_images = lax.psum_scatter(
        image_terms.astype(jnp.bfloat16), "seq", scatter_dimension=2, tiled=True
    ).astype(jnp.float32)
    grad_cross_kv = jnp.zeros((model_width, 2 * model_width), jnp.float32)
    grad_cross_kv = lax.dynamic_update_slice_in_dim(
        grad_cross_kv, grad_local_pairs[:, :head_span], seq_index * head_span, 1
    )
    grad_cross_kv = lax.dynamic_update_slice_in_dim(
        grad_cross_kv, grad_local_pairs[:, head_span:], model_width + seq_index * head_span, 1
    )
    query_grad_back = lax.all_to_all(
        grad_cross_queries.reshape(back_shape), "seq", split_axis=0, concat_axis=2, tiled=True
    )
    query_grad_tokens = query_grad_back.reshape(token_shape)
    grad_cross_q = weight_grad(normed_two, query_grad_tokens)
    grad_normed_two = linear_back(query_grad_tokens, full_cross_q)
    norm_grad_two, grad_gain_two = norm_back(
        after_self, gain_two.astype(jnp.float32), grad_normed_two
    )
    grad_after_self = grad_after_cross + norm_grad_two
    self_branch = grad_after_self.astype(jnp.bfloat16)
    grad_self_out = weight_grad(self_tokens, self_branch)
    self_full_grad = linear_back(self_branch, full_self_out).astype(jnp.bfloat16)
    self_upstream = lax.all_to_all(
        self_full_grad.reshape(split_shape), "seq", split_axis=2, concat_axis=0, tiled=True
    ).reshape(head_shape)
    grad_queries, grad_keys, grad_values = attend_back(
        query_heads, key_heads, value_heads, causal, factor, self_totals, self_upstream
    )
    query_back, key_back, value_back = (
        lax.all_to_all(
            grad_queries.reshape(back_shape), "seq", split_axis=0, concat_axis=2, tiled=True
        ),
        lax.all_to_all(
            grad_keys.reshape(back_shape), "seq", split_axis=0, concat_axis=2, tiled=True
        ),
        lax.all_to_all(
            grad_values.reshape(back_shape), "seq", split_axis=0, concat_axis=2, tiled=True
        ),
    )
    packed_grad = jnp.concatenate(
        [
            query_back.reshape(token_shape),
            key_back.reshape(token_shape),
            value_back.reshape(token_shape),
        ],
        axis=-1,
    )
    grad_qkv = weight_grad(normed_one, packed_grad)
    grad_normed_one = linear_back(packed_grad, full_qkv)
    norm_grad_one, grad_gain_one = norm_back(tokens, gain_one.astype(jnp.float32), grad_normed_one)
    grad_captions = grad_after_self + norm_grad_one
    shards = (
        lax.psum_scatter(grad_gain_one, ("dp", "seq"), scatter_dimension=0, tiled=True),
        lax.psum_scatter(grad_gain_two, ("dp", "seq"), scatter_dimension=0, tiled=True),
        lax.psum_scatter(grad_gain_three, ("dp", "seq"), scatter_dimension=0, tiled=True),
        lax.psum_scatter(grad_qkv, ("dp", "seq"), scatter_dimension=0, tiled=True),
        lax.psum_scatter(grad_self_out, ("dp", "seq"), scatter_dimension=0, tiled=True),
        lax.psum_scatter(grad_cross_q, ("dp", "seq"), scatter_dimension=0, tiled=True),
        lax.psum_scatter(grad_cross_kv, ("dp", "seq"), scatter_dimension=0, tiled=True),
        lax.psum_scatter(grad_cross_out, ("dp", "seq"), scatter_dimension=0, tiled=True),
        lax.psum_scatter(grad_up, ("dp", "seq"), scatter_dimension=0, tiled=True),
        lax.psum_scatter(grad_down, ("dp", "seq"), scatter_dimension=0, tiled=True),
    )
    return (
        block_out,
        grad_captions,
        grad_images,
        shards[0],
        shards[1],
        shards[2],
        shards[3],
        shards[4],
        shards[5],
        shards[6],
        shards[7],
        shards[8],
        shards[9],
    )


def solution(mesh):
    return jax.shard_map(
        on_device,
        mesh=mesh,
        in_specs=(
            P(("dp", "seq"), None, None),
            P("dp", None, None),
            P("dp", None),
            P(("dp", "seq")),
            P(("dp", "seq")),
            P(("dp", "seq")),
            P(("dp", "seq"), None),
            P(("dp", "seq"), None),
            P(("dp", "seq"), None),
            P(("dp", "seq"), None),
            P(("dp", "seq"), None),
            P(("dp", "seq"), None),
            P(("dp", "seq"), None),
            P(("dp", "seq"), None, None),
        ),
        out_specs=(
            P(("dp", "seq"), None, None),
            P(("dp", "seq"), None, None),
            P("dp", None, "seq"),
            P(("dp", "seq")),
            P(("dp", "seq")),
            P(("dp", "seq")),
            P(("dp", "seq"), None),
            P(("dp", "seq"), None),
            P(("dp", "seq"), None),
            P(("dp", "seq"), None),
            P(("dp", "seq"), None),
            P(("dp", "seq"), None),
            P(("dp", "seq"), None),
        ),
        check_vma=False,
    )
```

profile of v0, /device:TPU:0, one launch (start us, length us, event | category | flops | bytes accessed | tf_op | source)
XLA Modules:
  0.0 1383.9 jit_solution(16979897317913632275)
XLA Ops:
  13.7 42.1 %all-reduce.7 = (bf16[768]{0:T(1024)(128)(2,1)S(1)}, bf16[768]{0:T(1024)(128)(2,1)}, bf16[768]{0:T(1024)(128)(2,1)}) all-reduce(bf16[768]{0:T(1024)(128)(2,1)S(1)} %dynamic-update-slice, bf16[768]{0:T(1024)(128)(2,1)S(1)} %dynamic-update-slice.1, bf16[768]{0:T(1024)(128)(2,1)S(1)} %dynamic-update-slice.2), channel_id=1, replica_groups=mesh['dp'=8,'seq'=4] {'dp','seq'}, use_global_device_ids=true, to_apply=%add | all-reduce | flops 2304 | bytes 9216
  58.6 15.4 %all-gather.8.cloned.1.call-done = bf16[768,2304]{1,0:T(8,128)(2,1)} async-done(((bf16[24,2304]{1,0:T(8,128)(2,1)}), bf16[768,2304]{1,0:T(8,128)(2,1)}) %all-gather.8.cloned.1.call-update) | async-done | bytes 3538960 | tf_op jit(solution)/shard_map/all_gather | solution.py:120
  83.8 8.9 all-to-all-done.2
  98.7 8.0 all-to-all-done.1
  106.8 4.1 all-to-all-start
  113.3 8.1 all-to-all-done
  127.5 5.8 all-gather.12.cloned.1.call-done
  137.1 52.2 %all-gather.10.cloned.1.call-done = bf16[768,768]{1,0:T(8,128)(2,1)} async-done(((bf16[24,768]{1,0:T(8,128)(2,1)}), bf16[768,768]{1,0:T(8,128)(2,1)}) %all-gather.10.cloned.1.call-update) | async-done | bytes 1179664 | tf_op jit(solution)/shard_map/all_gather | solution.py:121
  191.6 53.5 %all-gather.14.cloned.1.call-done = bf16[768,768]{1,0:T(8,128)(2,1)} async-done(((bf16[24,768]{1,0:T(8,128)(2,1)}), bf16[768,768]{1,0:T(8,128)(2,1)}) %all-gather.14.cloned.1.call-update) | async-done | bytes 1179664 | tf_op jit(solution)/shard_map/all_gather | solution.py:122
  248.2 4.4 all-to-all-start.4
  252.6 4.2 convert_bitcast_fusion
  269.2 3.9 all-to-all-start.5
  273.1 9.5 all-to-all-done.5
  282.6 18.4 %all-gather.16.cloned.1.call-done = bf16[768,768]{1,0:T(8,128)(2,1)} async-done(((bf16[24,768]{1,0:T(8,128)(2,1)}), bf16[768,768]{1,0:T(8,128)(2,1)}) %all-gather.16.cloned.1.call-update) | async-done | bytes 1179664 | tf_op jit(solution)/shard_map/all_gather | solution.py:124
  305.0 61.3 %all-gather.18.cloned.1.call-done = bf16[768,3072]{1,0:T(8,128)(2,1)} async-done(((bf16[24,3072]{1,0:T(8,128)(2,1)}), bf16[768,3072]{1,0:T(8,128)(2,1)}) %all-gather.18.cloned.1.call-update) | async-done | bytes 4718608 | tf_op jit(solution)/shard_map/all_gather | solution.py:125
  366.3 5.7 fusion.101
  374.2 11.6 multiply_convert_fusion
  385.8 45.8 %all-gather.20.cloned.1.call-done = bf16[3072,768]{1,0:T(8,128)(2,1)} async-done(((bf16[96,768]{1,0:T(8,128)(2,1)}), bf16[3072,768]{1,0:T(8,128)(2,1)}) %all-gather.20.cloned.1.call-update) | async-done | bytes 4718608 | tf_op jit(solution)/shard_map/all_gather | solution.py:126
  431.6 8.2 add_convert_fusion
  439.8 6.0 multiply_reduce_fusion.2
  455.8 8.5 all-to-all-done.6
  464.3 4.4 fusion.134
  471.0 8.2 fusion.57
  483.4 6.7 convolution_convert_fusion.1
  493.6 9.2 fusion.69
  502.8 17.0 %all_to_all.180 = bf16[12,128,1,192]{1,3,2,0:T(8,128)(2,1)S(1)} all-to-all(bf16[12,128,1,192]{1,3,2,0:T(8,128)(2,1)S(1)} %bitcast.236), channel_id=1, replica_groups=mesh['dp'=8,'seq'=4] {'seq'}, dimensions={0} | all-to-all | bytes 1179648 | tf_op jit(solution)/shard_map/all_to_all | solution.py:252
  529.4 4.7 convolution_bitcast_fusion.6
  538.3 4.9 dynamic_update_slice.6
  543.3 4.8 dynamic_update_slice.7
  556.2 8.1 all-to-all-done.8
  567.3 4.6 fusion.75
  571.9 4.2 all-to-all-start.9
  576.1 4.5 fusion.78
  580.6 5.1 all-to-all-done.9
  585.7 4.1 all-to-all-start.10
  592.3 9.7 all-to-all-done.10
  608.6 6.5 all-to-all-done.11
  615.3 5.1 convolution_bitcast_fusion
  621.7 6.9 convolution_bitcast_fusion.2
  629.7 8.0 convolution_bitcast_fusion.1
  637.8 6.0 fusion.72
  646.1 41.3 %all-reduce.6 = (f32[768]{0:T(1024)S(1)}, f32[768]{0:T(1024)S(1)}, f32[768]{0:T(1024)S(1)}) all-reduce(f32[768]{0:T(1024)S(1)} %get-tuple-element.19, f32[768]{0:T(1024)} %get-tuple-element.15, f32[768]{0:T(1024)} %get-tuple-element.17), channel_id=3, replica_groups=mesh['dp'=8,'seq'=4] {'dp','seq'}, use_global_device_ids=true, to_apply=%region_20.21.clone | all-reduce | flops 2304 | bytes 18432
  693.6 58.0 %reduce-scatter.15.cloned.1.call-done = f32[24,768]{1,0:T(8,128)} async-done(((f32[768,768]{1,0:T(8,128)}), f32[24,768]{1,0:T(8,128)}) %reduce-scatter.15.cloned.1.call-update) | async-done | bytes 73744 | tf_op jit(solution)/shard_map/reduce_scatter | solution.py:300
  751.6 104.8 %reduce-scatter.13.cloned.1.call-done = f32[24,768]{1,0:T(8,128)} async-done(((f32[768,768]{1,0:T(8,128)}), f32[24,768]{1,0:T(8,128)}) %reduce-scatter.13.cloned.1.call-update) | async-done | bytes 73744 | tf_op jit(solution)/shard_map/reduce_scatter | solution.py:299
  856.4 111.9 %reduce-scatter.17.cloned.1.call-done = f32[24,1536]{1,0:T(8,128)} async-done(((f32[768,1536]{1,0:T(8,128)}), f32[24,1536]{1,0:T(8,128)}) %reduce-scatter.17.cloned.1.call-update) | async-done | bytes 147472 | tf_op jit(solution)/shard_map/reduce_scatter | solution.py:301
  968.3 125.6 %reduce-scatter.11.cloned.1.call-done = f32[24,2304]{1,0:T(8,128)} async-done(((f32[768,2304]{1,0:T(8,128)}), f32[24,2304]{1,0:T(8,128)}) %reduce-scatter.11.cloned.1.call-update) | async-done | bytes 221200 | tf_op jit(solution)/shard_map/reduce_scatter | solution.py:298
  1093.9 141.2 %reduce-scatter.21.cloned.1.call-done = f32[24,3072]{1,0:T(8,128)} async-done(((f32[768,3072]{1,0:T(8,128)}), f32[24,3072]{1,0:T(8,128)}) %reduce-scatter.21.cloned.1.call-update) | async-done | bytes 294928 | tf_op jit(solution)/shard_map/reduce_scatter | solution.py:303
  1235.1 141.9 %reduce-scatter.23.cloned.1.call-done = f32[96,768]{1,0:T(8,128)} async-done(((f32[3072,768]{1,0:T(8,128)}), f32[96,768]{1,0:T(8,128)}) %reduce-scatter.23.cloned.1.call-update) | async-done | bytes 294928 | tf_op jit(solution)/shard_map/reduce_scatter | solution.py:304
  (257 shorter events, 125.8 us)
Async XLA Ops:
  7.2 66.8 %all-gather.8.cloned.1.call-start = ((), (), s32[]{:S(2)}) async-start(), calls=%async_computation.20 | async-start | bytes 3649536 | tf_op jit(solution)/shard_map/all_gather | solution.py:120
  7.9 125.4 %all-gather.12.cloned.1.call-start = ((), (), s32[]{:S(2)}) async-start(), calls=%async_computation.22 | async-start | bytes 2433024 | tf_op jit(solution)/shard_map/all_gather | solution.py:123
  8.7 180.6 %all-gather.10.cloned.1.call-start = ((), (), s32[]{:S(2)}) async-start(), calls=%async_computation.21 | async-start | bytes 1216512 | tf_op jit(solution)/shard_map/all_gather | solution.py:121
  9.4 235.7 %all-gather.14.cloned.1.call-start = ((), (), s32[]{:S(2)}) async-start(), calls=%async_computation.23 | async-start | bytes 1216512 | tf_op jit(solution)/shard_map/all_gather | solution.py:122
  10.0 291.0 %all-gather.16.cloned.1.call-start = ((), (), s32[]{:S(2)}) async-start(), calls=%async_computation.24 | async-start | bytes 1216512 | tf_op jit(solution)/shard_map/all_gather | solution.py:124
  10.6 355.7 %all-gather.18.cloned.1.call-start = ((), (), s32[]{:S(2)}) async-start(), calls=%async_computation.25 | async-start | bytes 4866048 | tf_op jit(solution)/shard_map/all_gather | solution.py:125
  58.6 19.3 %copy-start.51 = (f32[3,128]{1,0:T(4,128)}, f32[3,128]{1,0:T(4,128)S(1)}, u32[]{:S(2)}) copy-start(f32[3,128]{1,0:T(4,128)S(1)} %fusion.83) | copy-start | bytes 4612
  79.2 13.5 all-to-all-start.2
  92.7 18.2 %copy-start.25 = (bf16[3,128,4,192]{1,3,0,2:T(8,128)(2,1)}, bf16[3,128,4,192]{1,3,0,2:T(8,128)(2,1)S(1)}, u32[]{:S(2)}) copy-start(bf16[3,128,4,192]{1,3,0,2:T(8,128)(2,1)S(1)} %all-to-all-done.2) | copy-start | bytes 1769476
  92.7 14.1 %all-to-all-start.1 = ((bf16[3,128,4,192]{1,3,0,2:T(8,128)(2,1)}), bf16[3,128,4,192]{1,3,0,2:T(8,128)(2,1)S(1)}, u32[]{:S(2)}, u32[]{:S(2)}) async-start(bf16[3,128,4,192]{1,3,0,2:T(8,128)(2,1)} %copy.138), calls=%async_computation.1 | async-start | bytes 1179648 | tf_op jit(solution)/shard_map/all_to_all | solution.py:153
  96.2 335.4 %all-gather.20.cloned.1.call-start = ((), (), s32[]{:S(2)}) async-start(), calls=%async_computation.26 | async-start | bytes 4866048 | tf_op jit(solution)/shard_map/all_gather | solution.py:126
  106.8 14.7 %all-to-all-start = ((bf16[3,128,4,192]{1,3,0,2:T(8,128)(2,1)}), bf16[3,128,4,192]{1,3,0,2:T(8,128)(2,1)}, u32[]{:S(2)}, u32[]{:S(2)}) async-start(bf16[3,128,4,192]{1,3,0,2:T(8,128)(2,1)} %copy.136), calls=%async_computation | async-start | bytes 1179648 | tf_op jit(solution)/shard_map/all_to_all | solution.py:155
  112.3 11.6 copy-start.3
  113.3 8.1 copy-start.37
  123.9 65.4 %copy-start.2 = (bf16[3,128,768]{2,1,0:T(8,128)(2,1)S(1)}, bf16[3,128,768]{2,1,0:T(8,128)(2,1)}, u32[]{:S(2)}) copy-start(bf16[3,128,768]{2,1,0:T(8,128)(2,1)} %param.14) | copy-start | bytes 1769476
  123.9 13.1 all-to-all-start.3
  127.5 117.6 %copy-start.34 = (f32[768]{0:T(1024)}, f32[768]{0:T(1024)S(1)}, u32[]{:S(2)}) copy-start(f32[768]{0:T(1024)S(1)} %convert_element_type.141) | copy-start | bytes 9220
  135.7 116.9 %copy-start.30 = (bf16[768,192]{1,0:T(8,128)(2,1)}, bf16[768,192]{1,0:T(8,128)(2,1)S(1)}, u32[]{:S(2)}) copy-start(bf16[768,192]{1,0:T(8,128)(2,1)S(1)} %get-tuple-element.31) | copy-start | bytes 884740
  137.0 54.5 %copy-start.14 = (bf16[3,128,4,1,192]{1,4,2,0,3:T(8,128)(2,1)}, bf16[3,128,4,1,192]{1,4,2,0,3:T(8,128)(2,1)S(1)}, u32[]{:S(2)}) copy-start(bf16[3,128,4,1,192]{1,4,2,0,3:T(8,128)(2,1)S(1)} %copy.143) | copy-start | bytes 1769476
  191.3 56.1 %copy-start.43 = (f32[3,128]{1,0:T(4,128)}, f32[3,128]{1,0:T(4,128)S(1)}, u32[]{:S(2)}) copy-start(f32[3,128]{1,0:T(4,128)S(1)} %broadcast_multiply_fusion.1) | copy-start | bytes 4612
  191.5 56.7 %copy-start.53 = (f32[3,128]{1,0:T(4,128)}, f32[3,128]{1,0:T(4,128)S(1)}, u32[]{:S(2)}) copy-start(f32[3,128]{1,0:T(4,128)S(1)} %multiply_reduce_fusion.7) | copy-start | bytes 4612
  191.6 56.6 %copy-start.48 = (f32[3,128]{1,0:T(4,128)}, f32[3,128]{1,0:T(4,128)S(1)}, u32[]{:S(2)}) copy-start(f32[3,128]{1,0:T(4,128)S(1)} %fusion.110) | copy-start | bytes 4612
  248.2 14.2 %all-to-all-start.4 = ((bf16[3,128,4,192]{1,3,0,2:T(8,128)(2,1)}), bf16[3,128,4,192]{1,3,0,2:T(8,128)(2,1)}, u32[]{:S(2)}, u32[]{:S(2)}) async-start(bf16[3,128,4,192]{1,3,0,2:T(8,128)(2,1)} %copy.147), calls=%async_computation.4 | async-start | bytes 1179648 | tf_op jit(solution)/shard_map/all_to_all | solution.py:168
  269.2 13.4 all-to-all-start.5
  303.0 142.8 %copy-start.5 = (f32[3,128,768]{2,1,0:T(8,128)}, f32[3,128,768]{2,1,0:T(8,128)S(1)}, u32[]{:S(2)}) copy-start(f32[3,128,768]{2,1,0:T(8,128)S(1)} %get-tuple-element.47) | copy-start | bytes 3538948
  431.6 8.2 copy-start.41
  431.6 8.2 copy-start.46
  451.3 13.0 all-to-all-start.6
  454.7 235.9 %reduce-scatter.9.cloned.1.call-start = ((), (), s32[]{:S(2)}) async-start(), calls=%async_computation.27 | async-start | bytes 5898240 | tf_op jit(solution)/shard_map/reduce_scatter | solution.py:242
  455.7 15.3 %copy-start.39 = (f32[12,3,128]{2,1,0:T(4,128)}, f32[12,3,128]{2,1,0:T(4,128)S(1)}, u32[]{:S(2)}) copy-start(f32[12,3,128]{2,1,0:T(4,128)S(1)} %log_add_fusion.1) | copy-start | bytes 55300
  490.1 203.5 %reduce-scatter.19.cloned.1.call-start = ((), (), s32[]{:S(2)}) async-start(), calls=%async_computation.32 | async-start | bytes 2433024 | tf_op jit(solution)/shard_map/reduce_scatter | solution.py:302
  493.5 258.1 %reduce-scatter.15.cloned.1.call-start = ((), (), s32[]{:S(2)}) async-start(), calls=%async_computation.30 | async-start | bytes 2433024 | tf_op jit(solution)/shard_map/reduce_scatter | solution.py:300
  502.8 17.1 %copy-start.35 = (f32[768]{0:T(1024)S(1)}, f32[768]{0:T(1024)}, u32[]{:S(2)}) copy-start(f32[768]{0:T(1024)} %copy-done.34) | copy-start | bytes 9220
  502.8 17.1 %copy-start.44 = (f32[3,128]{1,0:T(4,128)S(1)}, f32[3,128]{1,0:T(4,128)}, u32[]{:S(2)}) copy-start(f32[3,128]{1,0:T(4,128)} %copy-done.43) | copy-start | bytes 4612
  502.8 17.1 %copy-start.49 = (f32[3,128]{1,0:T(4,128)S(1)}, f32[3,128]{1,0:T(4,128)}, u32[]{:S(2)}) copy-start(f32[3,128]{1,0:T(4,128)} %copy-done.48) | copy-start | bytes 4612
  522.3 334.1 %reduce-scatter.13.cloned.1.call-start = ((), (), s32[]{:S(2)}) async-start(), calls=%async_computation.29 | async-start | bytes 2433024 | tf_op jit(solution)/shard_map/reduce_scatter | solution.py:299
  527.1 21.0 %copy-start.7 = (f32[3,128,768]{2,1,0:T(8,128)}, f32[3,128,768]{2,1,0:T(8,128)S(1)}, u32[]{:S(2)}) copy-start(f32[3,128,768]{2,1,0:T(8,128)S(1)} %add_add_fusion.4) | copy-start | bytes 3538948
  529.3 439.0 %reduce-scatter.17.cloned.1.call-start = ((), (), s32[]{:S(2)}) async-start(), calls=%async_computation.31 | async-start | bytes 4866048 | tf_op jit(solution)/shard_map/reduce_scatter | solution.py:301
  551.1 16.2 %copy-start.4 = (f32[12,3,128,128]{2,3,1,0:T(8,128)S(1)}, f32[12,3,128,128]{2,3,1,0:T(8,128)}, u32[]{:S(2)}) copy-start(f32[12,3,128,128]{2,3,1,0:T(8,128)} %copy-done.3) | copy-start | bytes 7077892
  551.2 13.1 all-to-all-start.8
  571.9 13.8 all-to-all-start.9
  585.7 16.3 %all-to-all-start.10 = ((bf16[12,128,1,192]{1,3,2,0:T(8,128)(2,1)}), bf16[12,128,1,192]{1,3,2,0:T(8,128)(2,1)}, u32[]{:S(2)}, u32[]{:S(2)}) async-start(bf16[12,128,1,192]{1,3,2,0:T(8,128)(2,1)} %bitcast.234), calls=%async_computation.10 | async-start | bytes 1179648 | tf_op jit(solution)/shard_map/all_to_all | solution.py:275
  602.0 13.0 all-to-all-start.11
  605.5 488.3 %reduce-scatter.11.cloned.1.call-start = ((), (), s32[]{:S(2)}) async-start(), calls=%async_computation.28 | async-start | bytes 7299072 | tf_op jit(solution)/shard_map/reduce_scatter | solution.py:298
  608.5 11.9 copy-start.21
  620.5 614.6 %reduce-scatter.21.cloned.1.call-start = ((), (), s32[]{:S(2)}) async-start(), calls=%async_computation.33 | async-start | bytes 9732096 | tf_op jit(solution)/shard_map/reduce_scatter | solution.py:303
  628.7 748.3 %reduce-scatter.23.cloned.1.call-start = ((), (), s32[]{:S(2)}) async-start(), calls=%async_computation.34 | async-start | bytes 9732096 | tf_op jit(solution)/shard_map/reduce_scatter | solution.py:304
  645.5 43.7 %copy-start.8 = (f32[3,128,768]{2,1,0:T(8,128)S(1)}, f32[3,128,768]{2,1,0:T(8,128)}, u32[]{:S(2)}) copy-start(f32[3,128,768]{2,1,0:T(8,128)} %copy-done.7) | copy-start | bytes 3538948
  (41 other events, 133.2 us)
Sparse Core Ops, SparseCore 0:
  10.9 63.0 all-gather.7
  76.9 56.3 all-gather.11
  136.2 52.9 all-gather.9
  192.0 53.0 all-gather.13
  247.8 53.0 all-gather.15
  303.7 62.5 all-gather.17
  369.2 62.3 all-gather.19
  490.2 51.1 reduce-scatter.8
  548.2 99.5 reduce-scatter.18
  653.5 98.0 reduce-scatter.14
  758.3 98.0 reduce-scatter.12
  862.3 105.9 reduce-scatter.16
  975.5 118.3 reduce-scatter.10
  1100.2 134.8 reduce-scatter.20
  1242.4 134.4 reduce-scatter.22
where the time goes:
time: 1390 us; the launch traced here: 1380 us
  waiting for transfers between devices  1010 us (73%)
  matrix products  132 us (9%)
  blocking collectives  100 us (7%)
  local copies, waits for them, and re-layouts  52.1 us (4%)
  starting transfers between devices  43.1 us (3%)
  other arithmetic  26.8 us (2%)
  between operations  15.3 us (1%)
    reduce_scatter x1, waiting for transfers between devices, on_device(): lax.psum_scatter(grad_down, ('dp', 'seq'), scatter_dimension=0, tiled=True)  142 us
    reduce_scatter x1, waiting for transfers between devices, on_device(): lax.psum_scatter(grad_up, ('dp', 'seq'), scatter_dimension=0, tiled=True)  141 us
    reduce_scatter x1, waiting for transfers between devices, on_device(): lax.psum_scatter(grad_qkv, ('dp', 'seq'), scatter_dimension=0, tiled=True)  126 us
    reduce_scatter x1, waiting for transfers between devices, on_device(): lax.psum_scatter(grad_cross_kv, ('dp', 'seq'), scatter_dimension=0, tiled...  112 us
    reduce_scatter x1, waiting for transfers between devices, on_device(): lax.psum_scatter(grad_self_out, ('dp', 'seq'), scatter_dimension=0, tiled...  105 us
    unnamed x2, blocking collectives  83.5 us
    all_gather x1, waiting for transfers between devices, on_device(): lax.all_gather(w_up, ('dp', 'seq'), axis=0, tiled=True)  61.3 us
    reduce_scatter x1, waiting for transfers between devices, on_device(): lax.psum_scatter(grad_cross_q, ('dp', 'seq'), scatter_dimension=0, tiled=...  58 us
  transfers between devices with their start and end apart: 26, of which 24 were waited for; matrix products, arithmetic and copies ran while one was open for 11% of the time, Pallas kernels for 0%

commit v1 on v0

--- a/solution.py
+++ b/solution.py
@@ -6,6 +6,18 @@
 HEADS = 12
 HEAD = 64
 epsilon = 1e-05
+
+
+def doubled_up(x, axis, dim):
+    ways, here = (lax.axis_size(axis), lax.axis_index(axis))
+    grown, reach = (x, 1)
+    while reach < ways:
+        theirs = lax.ppermute(grown, axis, [(d, d ^ reach) for d in range(ways)])
+        mine_first = jnp.concatenate([grown, theirs], axis=dim)
+        theirs_first = jnp.concatenate([theirs, grown], axis=dim)
+        grown = jnp.where(here & reach == 0, mine_first, theirs_first)
+        reach = 2 * reach
+    return grown
 
 
 def layer_norm(inputs, gain_vector):
@@ -119,7 +131,7 @@
         lax.all_gather(gain_mlp, ("dp", "seq"), axis=0, tiled=True),
         lax.all_gather(w_qkv, ("dp", "seq"), axis=0, tiled=True),
         lax.all_gather(w_self_out, ("dp", "seq"), axis=0, tiled=True),
-        lax.all_gather(w_cross_q, ("dp", "seq"), axis=0, tiled=True),
+        doubled_up(w_cross_q, ("dp", "seq"), 0),
         lax.all_gather(w_cross_kv, ("dp", "seq"), axis=0, tiled=True),
         lax.all_gather(w_cross_out, ("dp", "seq"), axis=0, tiled=True),
         lax.all_gather(w_up, ("dp", "seq"), axis=0, tiled=True),

time: 1390 us -> 1340 us (0.964)
  waiting for transfers between devices: 1010 us -> 953 us
    all_gather x1, waiting for transfers between devices: 53.5 us -> 0.02 us  [on_device(): lax.all_gather(w_cross_q, ('dp', 'seq'), axis=0, tiled=True)]
  transfers between devices with their start and end apart: 26 -> 31, of which waited for: 24 -> 24; matrix products, arithmetic and copies ran while one was open for 11% -> 16% of each run, Pallas kernels for 0% -> 0%
where the time goes in v1:
time: 1340 us; the launch traced here: 1330 us
  waiting for transfers between devices  953 us (71%)
  matrix products  134 us (10%)
  blocking collectives  101 us (8%)
  local copies, waits for them, and re-layouts  53.7 us (4%)
  starting transfers between devices  47.4 us (4%)
  other arithmetic  30.9 us (2%)
  between operations  15.3 us (1%)
    reduce_scatter x1, waiting for transfers between devices, on_device(): lax.psum_scatter(grad_down, ('dp', 'seq'), scatter_dimension=0, tiled=True)  142 us
    reduce_scatter x1, waiting for transfers between devices, on_device(): lax.psum_scatter(grad_up, ('dp', 'seq'), scatter_dimension=0, tiled=True)  141 us
    reduce_scatter x1, waiting for transfers between devices, on_device(): lax.psum_scatter(grad_qkv, ('dp', 'seq'), scatter_dimension=0, tiled=True)  126 us
    reduce_scatter x1, waiting for transfers between devices, on_device(): lax.psum_scatter(grad_cross_kv, ('dp', 'seq'), scatter_dimension=0, tiled...  112 us
    reduce_scatter x1, waiting for transfers between devices, on_device(): lax.psum_scatter(grad_self_out, ('dp', 'seq'), scatter_dimension=0, tiled...  105 us
    unnamed x2, blocking collectives  83.5 us
    all_gather x1, waiting for transfers between devices, on_device(): lax.all_gather(w_up, ('dp', 'seq'), axis=0, tiled=True)  61.3 us
    reduce_scatter x1, waiting for transfers between devices, on_device(): lax.psum_scatter(grad_cross_q, ('dp', 'seq'), scatter_dimension=0, tiled=...  57 us
  transfers between devices with their start and end apart: 31, of which 24 were waited for; matrix products, arithmetic and copies ran while one was open for 16% of the time, Pallas kernels for 0%

profile of v1, /device:TPU:0, one launch (start us, length us, event | category | flops | bytes accessed | tf_op | source)
XLA Modules:
  0.0 1334.7 jit_solution(1087082328544958652)
XLA Ops:
  13.7 42.1 %all-reduce.7 = (bf16[768]{0:T(1024)(128)(2,1)S(1)}, bf16[768]{0:T(1024)(128)(2,1)S(1)}, bf16[768]{0:T(1024)(128)(2,1)}) all-reduce(bf16[768]{0:T(1024)(128)(2,1)S(1)} %dynamic-update-slice, bf16[768]{0:T(1024)(128)(2,1)S(1)} %dynamic-update-slice.1, bf16[768]{0:T(1024)(128)(2,1)S(1)} %dynamic-update-slice.2), channel_id=1, replica_groups=mesh['dp'=8,'seq'=4] {'dp','seq'}, use_global_device_ids=true, to_apply=%add | all-reduce | flops 2304 | bytes 9216
  58.6 15.4 %all-gather.8.cloned.1.call-done = bf16[768,2304]{1,0:T(8,128)(2,1)} async-done(((bf16[24,2304]{1,0:T(8,128)(2,1)}), bf16[768,2304]{1,0:T(8,128)(2,1)}) %all-gather.8.cloned.1.call-update) | async-done | bytes 3538960 | tf_op jit(solution)/shard_map/all_gather | solution.py:132
  74.0 3.8 convolution_convert_fusion
  87.1 6.1 all-to-all-done.2
  98.8 4.7 collective-permute-done.2
  107.2 4.2 all-to-all-start
  113.8 8.3 all-to-all-done
  124.5 3.6 all-to-all-start.3
  137.7 54.6 %all-gather.10.cloned.1.call-done = bf16[768,768]{1,0:T(8,128)(2,1)} async-done(((bf16[24,768]{1,0:T(8,128)(2,1)}), bf16[768,768]{1,0:T(8,128)(2,1)}) %all-gather.10.cloned.1.call-update) | async-done | bytes 1179664 | tf_op jit(solution)/shard_map/all_gather | solution.py:133
  199.0 4.4 all-to-all-start.4
  203.4 4.2 convert_bitcast_fusion
  224.1 8.7 all-to-all-done.5
  232.9 15.3 %all-gather.14.cloned.1.call-done = bf16[768,768]{1,0:T(8,128)(2,1)} async-done(((bf16[24,768]{1,0:T(8,128)(2,1)}), bf16[768,768]{1,0:T(8,128)(2,1)}) %all-gather.14.cloned.1.call-update) | async-done | bytes 1179664 | tf_op jit(solution)/shard_map/all_gather | solution.py:136
  252.2 61.3 %all-gather.16.cloned.1.call-done = bf16[768,3072]{1,0:T(8,128)(2,1)} async-done(((bf16[24,3072]{1,0:T(8,128)(2,1)}), bf16[768,3072]{1,0:T(8,128)(2,1)}) %all-gather.16.cloned.1.call-update) | async-done | bytes 4718608 | tf_op jit(solution)/shard_map/all_gather | solution.py:137
  313.5 5.7 fusion.107
  321.5 11.6 multiply_convert_fusion
  333.1 45.6 %all-gather.18.cloned.1.call-done = bf16[3072,768]{1,0:T(8,128)(2,1)} async-done(((bf16[96,768]{1,0:T(8,128)(2,1)}), bf16[3072,768]{1,0:T(8,128)(2,1)}) %all-gather.18.cloned.1.call-update) | async-done | bytes 4718608 | tf_op jit(solution)/shard_map/all_gather | solution.py:138
  378.7 8.2 add_convert_fusion
  386.9 6.0 multiply_reduce_fusion.2
  402.9 9.0 all-to-all-done.6
  411.9 4.3 fusion.142
  416.2 8.3 fusion.57
  427.1 4.4 fusion.60
  434.0 6.5 convolution_convert_fusion.1
  444.0 9.1 fusion.69
  453.2 17.0 %all_to_all.180 = bf16[12,128,1,192]{1,3,2,0:T(8,128)(2,1)S(1)} all-to-all(bf16[12,128,1,192]{1,3,2,0:T(8,128)(2,1)S(1)} %bitcast.237), channel_id=1, replica_groups=mesh['dp'=8,'seq'=4] {'seq'}, dimensions={0} | all-to-all | bytes 1179648 | tf_op jit(solution)/shard_map/all_to_all | solution.py:264
  480.4 4.7 convolution_bitcast_fusion.6
  489.4 5.0 dynamic_update_slice.6
  494.3 4.8 dynamic_update_slice.7
  507.2 8.1 all-to-all-done.8
  518.4 4.6 fusion.75
  523.0 4.2 all-to-all-start.9
  527.2 4.5 fusion.78
  531.6 5.1 all-to-all-done.9
  536.8 4.1 all-to-all-start.10
  543.4 10.3 all-to-all-done.10
  560.3 6.5 all-to-all-done.11
  567.0 5.1 convolution_bitcast_fusion
  573.5 6.9 convolution_bitcast_fusion.2
  581.5 8.0 convolution_bitcast_fusion.1
  589.5 6.0 fusion.72
  597.9 41.4 %all-reduce.6 = (f32[768]{0:T(1024)S(1)}, f32[768]{0:T(1024)S(1)}, f32[768]{0:T(1024)S(1)}) all-reduce(f32[768]{0:T(1024)S(1)} %get-tuple-element.19, f32[768]{0:T(1024)} %get-tuple-element.15, f32[768]{0:T(1024)} %get-tuple-element.17), channel_id=3, replica_groups=mesh['dp'=8,'seq'=4] {'dp','seq'}, use_global_device_ids=true, to_apply=%region_20.21.clone | all-reduce | flops 2304 | bytes 18432
  645.4 57.0 %reduce-scatter.15.cloned.1.call-done = f32[24,768]{1,0:T(8,128)} async-done(((f32[768,768]{1,0:T(8,128)}), f32[24,768]{1,0:T(8,128)}) %reduce-scatter.15.cloned.1.call-update) | async-done | bytes 73744 | tf_op jit(solution)/shard_map/reduce_scatter | solution.py:312
  702.4 104.8 %reduce-scatter.13.cloned.1.call-done = f32[24,768]{1,0:T(8,128)} async-done(((f32[768,768]{1,0:T(8,128)}), f32[24,768]{1,0:T(8,128)}) %reduce-scatter.13.cloned.1.call-update) | async-done | bytes 73744 | tf_op jit(solution)/shard_map/reduce_scatter | solution.py:311
  807.2 111.9 %reduce-scatter.17.cloned.1.call-done = f32[24,1536]{1,0:T(8,128)} async-done(((f32[768,1536]{1,0:T(8,128)}), f32[24,1536]{1,0:T(8,128)}) %reduce-scatter.17.cloned.1.call-update) | async-done | bytes 147472 | tf_op jit(solution)/shard_map/reduce_scatter | solution.py:313
  919.1 125.5 %reduce-scatter.11.cloned.1.call-done = f32[24,2304]{1,0:T(8,128)} async-done(((f32[768,2304]{1,0:T(8,128)}), f32[24,2304]{1,0:T(8,128)}) %reduce-scatter.11.cloned.1.call-update) | async-done | bytes 221200 | tf_op jit(solution)/shard_map/reduce_scatter | solution.py:310
  1044.6 141.1 %reduce-scatter.21.cloned.1.call-done = f32[24,3072]{1,0:T(8,128)} async-done(((f32[768,3072]{1,0:T(8,128)}), f32[24,3072]{1,0:T(8,128)}) %reduce-scatter.21.cloned.1.call-update) | async-done | bytes 294928 | tf_op jit(solution)/shard_map/reduce_scatter | solution.py:315
  1185.8 141.9 %reduce-scatter.23.cloned.1.call-done = f32[96,768]{1,0:T(8,128)} async-done(((f32[3072,768]{1,0:T(8,128)}), f32[96,768]{1,0:T(8,128)}) %reduce-scatter.23.cloned.1.call-update) | async-done | bytes 294928 | tf_op jit(solution)/shard_map/reduce_scatter | solution.py:316
  (263 shorter events, 135.2 us)
Async XLA Ops:
  7.2 66.8 %all-gather.8.cloned.1.call-start = ((), (), s32[]{:S(2)}) async-start(), calls=%async_computation.20 | async-start | bytes 3649536 | tf_op jit(solution)/shard_map/all_gather | solution.py:132
  7.9 125.7 %all-gather.12.cloned.1.call-start = ((), (), s32[]{:S(2)}) async-start(), calls=%async_computation.22 | async-start | bytes 2433024 | tf_op jit(solution)/shard_map/all_gather | solution.py:135
  8.7 183.7 %all-gather.10.cloned.1.call-start = ((), (), s32[]{:S(2)}) async-start(), calls=%async_computation.21 | async-start | bytes 1216512 | tf_op jit(solution)/shard_map/all_gather | solution.py:133
  9.4 238.8 %all-gather.14.cloned.1.call-start = ((), (), s32[]{:S(2)}) async-start(), calls=%async_computation.23 | async-start | bytes 1216512 | tf_op jit(solution)/shard_map/all_gather | solution.py:136
  10.0 303.5 %all-gather.16.cloned.1.call-start = ((), (), s32[]{:S(2)}) async-start(), calls=%async_computation.24 | async-start | bytes 4866048 | tf_op jit(solution)/shard_map/all_gather | solution.py:137
  10.6 368.2 %all-gather.18.cloned.1.call-start = ((), (), s32[]{:S(2)}) async-start(), calls=%async_computation.25 | async-start | bytes 4866048 | tf_op jit(solution)/shard_map/all_gather | solution.py:138
  58.6 19.3 %copy-start.48 = (f32[3,128]{1,0:T(4,128)}, f32[3,128]{1,0:T(4,128)S(1)}, u32[]{:S(2)}) copy-start(f32[3,128]{1,0:T(4,128)S(1)} %fusion.83) | copy-start | bytes 4612
  79.2 14.0 %all-to-all-start.2 = ((bf16[3,128,4,192]{1,3,0,2:T(8,128)(2,1)}), bf16[3,128,4,192]{1,3,0,2:T(8,128)(2,1)S(1)}, u32[]{:S(2)}, u32[]{:S(2)}) async-start(bf16[3,128,4,192]{1,3,0,2:T(8,128)(2,1)} %copy.140), calls=%async_computation.2 | async-start | bytes 1179648 | tf_op jit(solution)/shard_map/all_to_all | solution.py:166
  82.7 1.4 collective-permute-start
  84.1 12.6 collective-permute-start.1
  93.2 18.2 %copy-start.22 = (bf16[3,128,4,192]{1,3,0,2:T(8,128)(2,1)}, bf16[3,128,4,192]{1,3,0,2:T(8,128)(2,1)S(1)}, u32[]{:S(2)}) copy-start(bf16[3,128,4,192]{1,3,0,2:T(8,128)(2,1)S(1)} %all-to-all-done.2) | copy-start | bytes 1769476
  93.2 14.1 %all-to-all-start.1 = ((bf16[3,128,4,192]{1,3,0,2:T(8,128)(2,1)}), bf16[3,128,4,192]{1,3,0,2:T(8,128)(2,1)S(1)}, u32[]{:S(2)}, u32[]{:S(2)}) async-start(bf16[3,128,4,192]{1,3,0,2:T(8,128)(2,1)} %copy.138), calls=%async_computation.1 | async-start | bytes 1179648 | tf_op jit(solution)/shard_map/all_to_all | solution.py:165
  96.7 6.8 collective-permute-start.2
  98.2 97.0 %copy-start.34 = (f32[768]{0:T(1024)}, f32[768]{0:T(1024)S(1)}, u32[]{:S(2)}) copy-start(f32[768]{0:T(1024)S(1)} %convert_element_type.141) | copy-start | bytes 9220
  104.3 24.5 %collective-permute-start.3 = (bf16[192,768]{1,0:T(8,128)(2,1)}, bf16[192,768]{1,0:T(8,128)(2,1)}, u32[]{:S(2)}, u32[]{:S(2)}) collective-permute-start(bf16[192,768]{1,0:T(8,128)(2,1)} %maximum_select_fusion.2), channel_id=1, source_target_pairs={{0,8},{1,9},{2,10},{3,11},{4,12},{5,13},{6,14},{7,15},{8,0},{9,1},... | collective-permute-start | bytes 884744 | tf_op jit(solution)/shard_map/ppermute | solution.py:15
  107.2 14.9 %all-to-all-start = ((bf16[3,128,4,192]{1,3,0,2:T(8,128)(2,1)}), bf16[3,128,4,192]{1,3,0,2:T(8,128)(2,1)}, u32[]{:S(2)}, u32[]{:S(2)}) async-start(bf16[3,128,4,192]{1,3,0,2:T(8,128)(2,1)} %copy.136), calls=%async_computation | async-start | bytes 1179648 | tf_op jit(solution)/shard_map/all_to_all | solution.py:167
  112.8 11.8 copy-start.2
  113.8 10.7 copy-start.36
  124.5 67.8 %copy-start.1 = (bf16[3,128,768]{2,1,0:T(8,128)(2,1)S(1)}, bf16[3,128,768]{2,1,0:T(8,128)(2,1)}, u32[]{:S(2)}) copy-start(bf16[3,128,768]{2,1,0:T(8,128)(2,1)} %param.14) | copy-start | bytes 1769476
  124.5 13.1 all-to-all-start.3
  130.2 65.0 %collective-permute-start.4 = (bf16[384,768]{1,0:T(8,128)(2,1)S(1)}, bf16[384,768]{1,0:T(8,128)(2,1)}, u32[]{:S(2)}, u32[]{:S(2)}) collective-permute-start(bf16[384,768]{1,0:T(8,128)(2,1)S(1)} %maximum_select_fusion.1), channel_id=1, source_target_pairs={{0,16},{1,17},{2,18},{3,19},{4,20},{5,21},{6,22},{7,23},{8,24},{9,... | collective-permute-start | bytes 1769480 | tf_op jit(solution)/shard_map/ppermute | solution.py:15
  137.7 56.9 %copy-start.12 = (bf16[3,128,4,1,192]{1,4,2,0,3:T(8,128)(2,1)}, bf16[3,128,4,1,192]{1,4,2,0,3:T(8,128)(2,1)S(1)}, u32[]{:S(2)}) copy-start(bf16[3,128,4,1,192]{1,4,2,0,3:T(8,128)(2,1)S(1)} %copy.143) | copy-start | bytes 1769476
  199.0 14.1 %all-to-all-start.4 = ((bf16[3,128,4,192]{1,3,0,2:T(8,128)(2,1)}), bf16[3,128,4,192]{1,3,0,2:T(8,128)(2,1)}, u32[]{:S(2)}, u32[]{:S(2)}) async-start(bf16[3,128,4,192]{1,3,0,2:T(8,128)(2,1)} %copy.147), calls=%async_computation.4 | async-start | bytes 1179648 | tf_op jit(solution)/shard_map/all_to_all | solution.py:180
  219.8 13.0 all-to-all-start.5
  223.3 249.6 %all-gather.20.cloned.1.call-start = ((), (), s32[]{:S(2)}) async-start(), calls=%async_computation.26 | async-start | bytes 1216512 | tf_op jit(solution)/shard_map/all_gather | solution.py:207
  250.2 142.7 %copy-start.4 = (f32[3,128,768]{2,1,0:T(8,128)}, f32[3,128,768]{2,1,0:T(8,128)S(1)}, u32[]{:S(2)}) copy-start(f32[3,128,768]{2,1,0:T(8,128)S(1)} %get-tuple-element.47) | copy-start | bytes 3538948
  378.7 8.2 copy-start.44
  398.4 13.5 %all-to-all-start.6 = ((bf16[3,128,4,192]{1,3,0,2:T(8,128)(2,1)}), bf16[3,128,4,192]{1,3,0,2:T(8,128)(2,1)S(1)}, u32[]{:S(2)}, u32[]{:S(2)}) async-start(bf16[3,128,4,192]{1,3,0,2:T(8,128)(2,1)} %copy.153), calls=%async_computation.6 | async-start | bytes 1179648 | tf_op jit(solution)/shard_map/all_to_all | solution.py:238
  401.9 240.5 %reduce-scatter.9.cloned.1.call-start = ((), (), s32[]{:S(2)}) async-start(), calls=%async_computation.27 | async-start | bytes 5898240 | tf_op jit(solution)/shard_map/reduce_scatter | solution.py:254
  402.9 24.1 %copy-start.38 = (f32[12,3,128]{2,1,0:T(4,128)}, f32[12,3,128]{2,1,0:T(4,128)S(1)}, u32[]{:S(2)}) copy-start(f32[12,3,128]{2,1,0:T(4,128)S(1)} %log_add_fusion.1) | copy-start | bytes 55300
  440.5 204.8 %reduce-scatter.19.cloned.1.call-start = ((), (), s32[]{:S(2)}) async-start(), calls=%async_computation.32 | async-start | bytes 2433024 | tf_op jit(solution)/shard_map/reduce_scatter | solution.py:314
  443.9 258.5 %reduce-scatter.15.cloned.1.call-start = ((), (), s32[]{:S(2)}) async-start(), calls=%async_computation.30 | async-start | bytes 2433024 | tf_op jit(solution)/shard_map/reduce_scatter | solution.py:312
  453.1 17.1 %copy-start.35 = (f32[768]{0:T(1024)S(1)}, f32[768]{0:T(1024)}, u32[]{:S(2)}) copy-start(f32[768]{0:T(1024)} %copy-done.34) | copy-start | bytes 9220
  453.1 17.1 %copy-start.43 = (f32[3,128]{1,0:T(4,128)S(1)}, f32[3,128]{1,0:T(4,128)}, u32[]{:S(2)}) copy-start(f32[3,128]{1,0:T(4,128)} %copy-done.42) | copy-start | bytes 4612
  453.1 17.1 %copy-start.47 = (f32[3,128]{1,0:T(4,128)S(1)}, f32[3,128]{1,0:T(4,128)}, u32[]{:S(2)}) copy-start(f32[3,128]{1,0:T(4,128)} %copy-done.46) | copy-start | bytes 4612
  472.7 334.5 %reduce-scatter.13.cloned.1.call-start = ((), (), s32[]{:S(2)}) async-start(), calls=%async_computation.29 | async-start | bytes 2433024 | tf_op jit(solution)/shard_map/reduce_scatter | solution.py:311
  478.2 21.0 %copy-start.6 = (f32[3,128,768]{2,1,0:T(8,128)}, f32[3,128,768]{2,1,0:T(8,128)S(1)}, u32[]{:S(2)}) copy-start(f32[3,128,768]{2,1,0:T(8,128)S(1)} %add_add_fusion.4) | copy-start | bytes 3538948
  480.4 438.7 %reduce-scatter.17.cloned.1.call-start = ((), (), s32[]{:S(2)}) async-start(), calls=%async_computation.31 | async-start | bytes 4866048 | tf_op jit(solution)/shard_map/reduce_scatter | solution.py:313
  502.2 16.2 %copy-start.3 = (f32[12,3,128,128]{2,3,1,0:T(8,128)S(1)}, f32[12,3,128,128]{2,3,1,0:T(8,128)}, u32[]{:S(2)}) copy-start(f32[12,3,128,128]{2,3,1,0:T(8,128)} %copy-done.2) | copy-start | bytes 7077892
  502.2 13.1 all-to-all-start.8
  523.0 13.8 %all-to-all-start.9 = ((bf16[12,128,1,192]{1,3,2,0:T(8,128)(2,1)}), bf16[12,128,1,192]{1,3,2,0:T(8,128)(2,1)}, u32[]{:S(2)}, u32[]{:S(2)}) async-start(bf16[12,128,1,192]{1,3,2,0:T(8,128)(2,1)} %bitcast.236), calls=%async_computation.9 | async-start | bytes 1179648 | tf_op jit(solution)/shard_map/all_to_all | solution.py:284
  536.8 17.0 %all-to-all-start.10 = ((bf16[12,128,1,192]{1,3,2,0:T(8,128)(2,1)}), bf16[12,128,1,192]{1,3,2,0:T(8,128)(2,1)}, u32[]{:S(2)}, u32[]{:S(2)}) async-start(bf16[12,128,1,192]{1,3,2,0:T(8,128)(2,1)} %bitcast.235), calls=%async_computation.10 | async-start | bytes 1179648 | tf_op jit(solution)/shard_map/all_to_all | solution.py:287
  553.7 13.0 all-to-all-start.11
  557.2 487.4 %reduce-scatter.11.cloned.1.call-start = ((), (), s32[]{:S(2)}) async-start(), calls=%async_computation.28 | async-start | bytes 7299072 | tf_op jit(solution)/shard_map/reduce_scatter | solution.py:310
  560.2 11.9 copy-start.18
  572.2 613.5 %reduce-scatter.21.cloned.1.call-start = ((), (), s32[]{:S(2)}) async-start(), calls=%async_computation.33 | async-start | bytes 9732096 | tf_op jit(solution)/shard_map/reduce_scatter | solution.py:315
  580.4 747.3 %reduce-scatter.23.cloned.1.call-start = ((), (), s32[]{:S(2)}) async-start(), calls=%async_computation.34 | async-start | bytes 9732096 | tf_op jit(solution)/shard_map/reduce_scatter | solution.py:316
  597.2 43.8 %copy-start.7 = (f32[3,128,768]{2,1,0:T(8,128)S(1)}, f32[3,128,768]{2,1,0:T(8,128)}, u32[]{:S(2)}) copy-start(f32[3,128,768]{2,1,0:T(8,128)} %copy-done.6) | copy-start | bytes 3538948
  (42 other events, 133.5 us)
Sparse Core Ops, SparseCore 0:
  10.9 63.0 all-gather.7
  76.9 56.6 all-gather.11
  136.5 55.7 all-gather.9
  195.1 53.0 all-gather.13
  251.0 62.5 all-gather.15
  316.3 62.3 all-gather.17
  381.6 52.9 all-gather.19
  440.6 51.1 reduce-scatter.8
  498.6 100.0 reduce-scatter.18
  604.4 97.9 reduce-scatter.14
  709.1 98.0 reduce-scatter.12
  813.1 105.9 reduce-scatter.16
  926.3 118.2 reduce-scatter.10
  1051.0 134.7 reduce-scatter.20
  1193.1 134.5 reduce-scatter.22
